TPU v7x, 32 devices: a whole 2x2x4 slice. The times are simulated.
32 devices in a mesh: row: 4 (over z), col: 8 (over y, x, core).
Axes of the slice: x: 2, y: 2, z: 4, core: 2. Of those that a mesh axis runs over, the one named last changes fastest.
Arguments:
- weight: float32 [16384, 16384], P('row', 'col'), may hold values from -0.046875 to 0.046875
- leak: float32 [16384], P('col'), may hold values from 0.1 to 1
- rates: float32 [3, 256, 16384], P(None, 'row', 'col'), may hold values from -0.95 to 0.95
- cotangent: float32 [256, 16384], P('row', 'col'), may hold values from -2 to 2
Outputs:
- grad_input: float32 [256, 16384], P('row', 'col')
- grad_weight: float32 [16384, 16384], P('row', 'col')
- grad_noise: float32 [3, 16384], P(None, 'row')
All inputs are finite; a program needn't handle non-finite values.
Results may differ from a plain program's by a relative error of at most 0.0001.
Values sent between devices are 32-bit elements; how exact they have to be, the bound alone decides.
A program may use at most 192 MiB of HBM per device.

v0:
```python
import jax
import jax.numpy as jnp
from jax import lax
from jax.sharding import PartitionSpec as P

TSTEPS = 3


def shards(weight, leak, rates, cotangent):
    n_col = lax.axis_size("col")
    own_rows = cotangent.shape[0]
    local_units = cotangent.shape[1]
    full_rates = lax.all_gather(rates, "row", axis=1, tiled=True)
    grad_weight = jnp.zeros(weight.shape, jnp.float32)
    noise_list = []
    carried = cotangent
    for step_back in range(TSTEPS - 1, -1, -1):
        scaled = leak[None, :] * carried
        spread = scaled.reshape(own_rows, local_units // n_col, n_col)
        by_col = lax.all_to_all(spread, "col", split_axis=2, concat_axis=1, tiled=True)
        by_row = lax.all_to_all(by_col, "row", split_axis=1, concat_axis=0, tiled=True)
        gathered = lax.all_gather(by_row, "col", axis=2, tiled=True)
        unit_block = gathered.reshape(gathered.shape[0], gathered.shape[1] * gathered.shape[2])
        rates_now = full_rates[step_back]
        noise_list.insert(0, jnp.sum(unit_block, axis=0))
        grad_weight = grad_weight + lax.dot_general(
            unit_block,
            rates_now,
            (((0,), (0,)), ((), ())),
            precision=lax.Precision.HIGHEST,
            preferred_element_type=jnp.float32,
        )
        partial_sum = jnp.dot(
            unit_block, weight, precision=lax.Precision.HIGHEST, preferred_element_type=jnp.float32
        )
        adjoint = lax.psum_scatter(partial_sum, "row", scatter_dimension=0, tiled=True)
        local_rates = rates[step_back]
        carried = (1.0 - leak[None, :]) * carried + (1.0 - local_rates * local_rates) * adjoint
    return (carried, grad_weight, jnp.stack(noise_list))


def solution(mesh):
    placed = (P("row", "col"), P("col"), P(None, "row", "col"), P("row", "col"))
    return jax.shard_map(
        shards,
        mesh=mesh,
        in_specs=placed,
        out_specs=(P("row", "col"), P("row", "col"), P(None, "row")),
        check_vma=False,
    )
```

profile of v0, /device:TPU:0, one launch (start us, length us, event | category | flops | bytes accessed | tf_op | source)
XLA Modules:
  0.0 634.5 jit_solution(5892808969612367369)
XLA Ops:
  9.0 14.7 %all_to_all.108 = f32[64,256,8]{1,0,2:T(8,128)S(1)} all-to-all(f32[64,256,8]{1,0,2:T(8,128)S(1)} %copy.20), channel_id=1, replica_groups=mesh['row'=4,'col'=8] {'col'}, dimensions={2} | all-to-all | bytes 1048576 | tf_op jit(solution)/shard_map/all_to_all | solution.py:20
  24.6 9.3 %reduce.3 = f32[2048,64]{1,0:T(8,128)S(1)} reduce(f32[2048,1,64]{2,1,0:T(1,128)S(1)} %bitcast.75, f32[]{:T(128)} %broadcast.24), dimensions={1}, to_apply=%bitcast.64.reduce_sub_computation | reduce | bytes 1048580
  34.6 18.6 %all_to_all.109 = f32[4,1,32768]{2,1,0:T(1,128)S(1)} all-to-all(f32[4,1,32768]{2,1,0:T(1,128)S(1)} %reshape.48), channel_id=1, replica_groups=mesh['row'=4,'col'=8] {'row'}, dimensions={0} | all-to-all | bytes 1048576 | tf_op jit(solution)/shard_map/all_to_all | solution.py:21
  53.2 2.1 reduce.4
  58.3 34.2 %all-gather.5.cloned.1.call-done = f32[256,512,8]{1,0,2:T(8,128)} async-done(((f32[256,512,1]{1,0,2:T(8,128)}), f32[256,512,8]{1,0,2:T(8,128)}) %all-gather.5.cloned.1.call-update) | async-done | bytes 4194320 | tf_op jit(solution)/shard_map/all_gather | solution.py:22
  92.6 5.4 copy.25
  98.0 33.9 %fusion.9 = f32[256,2048]{1,0:T(8,128)} fusion(f32[4096,2048]{1,0:T(8,128)} %param.4, f32[256,512,8]{0,2,1:T(8,128)} %copy.25), kind=kOutput, calls=%fused_computation.10 | convolution fusion | flops 25769803776 | bytes 39845888 | tf_op jit(solution)/shard_map/dot_general | solution.py:33
  132.0 43.7 %reduce-scatter.4.cloned.1.call-done = f32[64,2048]{1,0:T(8,128)} async-done(((f32[256,2048]{1,0:T(8,128)}), f32[64,2048]{1,0:T(8,128)}) %reduce-scatter.4.cloned.1.call-update) | async-done | bytes 524304 | tf_op jit(solution)/shard_map/reduce_scatter | solution.py:36
  177.7 13.7 %all_to_all.110 = f32[64,256,8]{1,0,2:T(8,128)S(1)} all-to-all(f32[64,256,8]{1,0,2:T(8,128)S(1)} %copy.27), channel_id=1, replica_groups=mesh['row'=4,'col'=8] {'col'}, dimensions={2} | all-to-all | bytes 1048576 | tf_op jit(solution)/shard_map/all_to_all | solution.py:20
  191.8 9.3 %reduce.5 = f32[2048,64]{1,0:T(8,128)S(1)} reduce(f32[2048,1,64]{2,1,0:T(1,128)S(1)} %bitcast.76, f32[]{:T(128)} %broadcast.24), dimensions={1}, to_apply=%bitcast.66.reduce_sub_computation | reduce | bytes 1048580
  201.8 16.6 %all_to_all.111 = f32[4,1,32768]{2,1,0:T(1,128)S(1)} all-to-all(f32[4,1,32768]{2,1,0:T(1,128)S(1)} %reshape.50), channel_id=1, replica_groups=mesh['row'=4,'col'=8] {'row'}, dimensions={0} | all-to-all | bytes 1048576 | tf_op jit(solution)/shard_map/all_to_all | solution.py:21
  218.4 2.1 reduce.6
  223.4 34.3 %all-gather.7.cloned.1.call-done = f32[256,512,8]{1,0,2:T(8,128)} async-done(((f32[256,512,1]{1,0,2:T(8,128)}), f32[256,512,8]{1,0,2:T(8,128)}) %all-gather.7.cloned.1.call-update) | async-done | bytes 4194320 | tf_op jit(solution)/shard_map/all_gather | solution.py:22
  257.7 5.5 copy.32
  263.2 33.8 %fusion.5 = f32[256,2048]{1,0:T(8,128)} fusion(f32[4096,2048]{1,0:T(8,128)} %param.4, f32[256,512,8]{0,2,1:T(8,128)} %copy.32), kind=kOutput, calls=%fused_computation.6 | convolution fusion | flops 25769803776 | bytes 39845888 | tf_op jit(solution)/shard_map/dot_general | solution.py:33
  297.8 43.2 %reduce-scatter.6.cloned.1.call-done = f32[64,2048]{1,0:T(8,128)} async-done(((f32[256,2048]{1,0:T(8,128)}), f32[64,2048]{1,0:T(8,128)}) %reduce-scatter.6.cloned.1.call-update) | async-done | bytes 524304 | tf_op jit(solution)/shard_map/reduce_scatter | solution.py:36
  340.9 2.0 broadcast_multiply_fusion
  343.7 13.5 %all_to_all.112 = f32[64,256,8]{1,0,2:T(8,128)} all-to-all(f32[64,256,8]{1,0,2:T(8,128)S(1)} %copy.34), channel_id=1, replica_groups=mesh['row'=4,'col'=8] {'col'}, dimensions={2} | all-to-all | bytes 1048576 | tf_op jit(solution)/shard_map/all_to_all | solution.py:20
  358.5 10.3 %reduce.7 = f32[2048,64]{1,0:T(8,128)} reduce(f32[2048,1,64]{2,1,0:T(1,128)S(1)} %bitcast.77, f32[]{:T(128)} %broadcast.24), dimensions={1}, to_apply=%bitcast.68.reduce_sub_computation | reduce | bytes 1048580
  368.9 1.9 reshape.52
  370.7 32.0 %all_to_all.113 = f32[4,1,32768]{2,1,0:T(1,128)S(1)} all-to-all(f32[4,1,32768]{2,1,0:T(1,128)S(1)} %reshape.52), channel_id=1, replica_groups=mesh['row'=4,'col'=8] {'row'}, dimensions={0} | all-to-all | bytes 1048576 | tf_op jit(solution)/shard_map/all_to_all | solution.py:21
  402.7 2.1 reduce.8
  407.8 2.6 reduce_sum.29
  410.7 57.2 %all-gather.11.cloned.1.call-done = f32[3,256,2048]{2,1,0:T(8,128)} async-done(((f32[3,64,2048]{2,1,0:T(8,128)}), f32[3,256,2048]{2,1,0:T(8,128)}) %all-gather.11.cloned.1.call-update) | async-done | bytes 6291472 | tf_op jit(solution)/shard_map/all_gather | solution.py:13
  468.0 32.4 %fusion.7 = f32[4096,2048]{1,0:T(8,128)} fusion(f32[256,512,8]{0,2,1:T(8,128)} %copy.25, f32[3,256,2048]{2,1,0:T(8,128)} %all-gather.11.cloned.1.call-done), kind=kOutput, calls=%fused_computation.8 | convolution fusion | flops 25769803776 | bytes 39845888 | tf_op jit(solution)/shard_map/dot_general | solution.py:26
  500.4 2.7 reduce_sum.28
  503.4 32.7 %fusion.3 = f32[4096,2048]{1,0:T(8,128)} fusion(f32[256,512,8]{0,2,1:T(8,128)} %copy.32, f32[3,256,2048]{2,1,0:T(8,128)} %all-gather.11.cloned.1.call-done), kind=kOutput, calls=%fused_computation.4 | convolution fusion | flops 25769803776 | bytes 39845888 | tf_op jit(solution)/shard_map/dot_general | solution.py:26
  536.0 2.6 reduce_sum.27
  539.0 5.5 copy.39
  544.4 33.9 %fusion.1 = f32[256,2048]{1,0:T(8,128)} fusion(f32[4096,2048]{1,0:T(8,128)} %param.4, f32[256,512,8]{0,2,1:T(8,128)} %copy.39), kind=kOutput, calls=%fused_computation.2 | convolution fusion | flops 25769803776 | bytes 39845888 | tf_op jit(solution)/shard_map/dot_general | solution.py:33
  579.1 46.4 %add_add_fusion = f32[4096,2048]{1,0:T(8,128)} fusion(f32[4096,2048]{1,0:T(8,128)} %fusion.7, f32[4096,2048]{1,0:T(8,128)} %fusion.3, f32[256,512,8]{0,2,1:T(8,128)} %copy.39, f32[3,256,2048]{2,1,0:T(8,128)} %all-gather.11.cloned.1.call-done), kind=kOutput, calls=%fused_computation | convolution fusion | flops 25786580992 | bytes 106954752 | tf_op jit(solution)/shard_map/dot_general | solution.py:26
  625.4 1.9 fusion.11
  (57 shorter events, 19.4 us)
Async XLA Ops:
  7.2 85.4 %all-gather.5.cloned.1.call-start = ((), (), s32[]{:S(2)}) async-start(), calls=%async_computation.9 | async-start | bytes 4718592 | tf_op jit(solution)/shard_map/all_gather | solution.py:22
  58.0 117.7 %reduce-scatter.4.cloned.1.call-start = ((), (), s32[]{:S(2)}) async-start(), calls=%async_computation.10 | async-start | bytes 2621440 | tf_op jit(solution)/shard_map/reduce_scatter | solution.py:36
  98.0 33.9 %copy-start.4 = (f32[2048]{0:T(1024)S(1)}, f32[2048]{0:T(1024)}, u32[]{:S(2)}) copy-start(f32[2048]{0:T(1024)} %param.5) | copy-start | bytes 24580
  98.0 77.7 %copy-start.1 = (f32[64,2048]{1,0:T(8,128)S(1)}, f32[64,2048]{1,0:T(8,128)}, u32[]{:S(2)}) copy-start(f32[64,2048]{1,0:T(8,128)} %param.7) | copy-start | bytes 1572868
  131.9 125.9 %all-gather.7.cloned.1.call-start = ((), (), s32[]{:S(2)}) async-start(), calls=%async_computation.11 | async-start | bytes 4718592 | tf_op jit(solution)/shard_map/all_gather | solution.py:22
  223.2 117.7 %reduce-scatter.6.cloned.1.call-start = ((), (), s32[]{:S(2)}) async-start(), calls=%async_computation.12 | async-start | bytes 2621440 | tf_op jit(solution)/shard_map/reduce_scatter | solution.py:36
  263.2 77.7 %copy-start.3 = (f32[64,2048]{1,0:T(8,128)S(1)}, f32[64,2048]{1,0:T(8,128)}, u32[]{:S(2)}) copy-start(f32[64,2048]{1,0:T(8,128)} %reduce-scatter.4.cloned.1.call-done) | copy-start | bytes 1572868
  297.1 43.8 %copy-start = (f32[3,64,2048]{2,1,0:T(8,128)S(1)}, f32[3,64,2048]{2,1,0:T(8,128)}, u32[]{:S(2)}) copy-start(f32[3,64,2048]{2,1,0:T(8,128)} %param.6) | copy-start | bytes 4718596
  297.1 170.9 %all-gather.11.cloned.1.call-start = ((), (), s32[]{:S(2)}) async-start(), calls=%async_computation.15 | async-start | bytes 7864320 | tf_op jit(solution)/shard_map/all_gather | solution.py:13
  297.7 238.3 %all-gather.9.cloned.1.call-start = ((), (), s32[]{:S(2)}) async-start(), calls=%async_computation.13 | async-start | bytes 4718592 | tf_op jit(solution)/shard_map/all_gather | solution.py:22
  407.5 217.9 %reduce-scatter.8.cloned.1.call-start = ((), (), s32[]{:S(2)}) async-start(), calls=%async_computation.14 | async-start | bytes 2621440 | tf_op jit(solution)/shard_map/reduce_scatter | solution.py:36
  579.1 46.4 %copy-start.2 = (f32[64,2048]{1,0:T(8,128)S(1)}, f32[64,2048]{1,0:T(8,128)}, u32[]{:S(2)}) copy-start(f32[64,2048]{1,0:T(8,128)} %get-tuple-element.4) | copy-start | bytes 1572868
Sparse Core Ops, SparseCore 0:
  58.1 34.4 all-gather.4
  132.0 43.6 reduce-scatter.3
  223.3 34.4 all-gather.6
  297.2 43.6 reduce-scatter.5
  342.3 125.6 all-gather.10
  469.7 34.7 all-gather.8
  578.5 41.7 reduce-scatter.7
where the time goes:
time: 642 us; the launch traced here: 634 us
  waiting for transfers between devices  213 us (33%)
  matrix products  213 us (33%)
  blocking collectives  109 us (17%)
  other arithmetic  50.4 us (8%)
  local copies, waits for them, and re-layouts  33 us (5%)
  between operations  14.6 us (2%)
    dot_general x3, matrix products, shards(): lax.dot_general(unit_block, rates_now, (((0,), (0,)), ((), ())), precisio...  111 us
    dot_general x3, matrix products, shards(): jnp.dot(unit_block, weight, precision=lax.Precision.HIGHEST, preferred_el...  102 us
    reduce_scatter x3, waiting for transfers between devices, shards(): lax.psum_scatter(partial_sum, 'row', scatter_dimension=0, tiled=True)  86.9 us
    all_gather x3, waiting for transfers between devices, shards(): gathered = lax.all_gather(by_row, 'col', axis=2, tiled=True)  68.6 us
    all_to_all x3, blocking collectives, shards(): lax.all_to_all(by_col, 'row', split_axis=1, concat_axis=0, tiled=True)  67.2 us
    all_gather x1, waiting for transfers between devices, shards(): full_rates = lax.all_gather(rates, 'row', axis=1, tiled=True)  57.2 us
    all_to_all x3, blocking collectives, shards(): lax.all_to_all(spread, 'col', split_axis=2, concat_axis=1, tiled=True)  41.9 us
    unnamed x3, other arithmetic  29 us
  transfers between devices with their start and end apart: 7, of which 5 were waited for; matrix products, arithmetic and copies ran while one was open for 22% of the time, Pallas kernels for 0%

commit v1 on v0

--- a/solution.py
+++ b/solution.py
@@ -19,7 +19,7 @@
         spread = scaled.reshape(own_rows, local_units // n_col, n_col)
         by_col = lax.all_to_all(spread, "col", split_axis=2, concat_axis=1, tiled=True)
         by_row = lax.all_to_all(by_col, "row", split_axis=1, concat_axis=0, tiled=True)
-        gathered = lax.all_gather(by_row, "col", axis=2, tiled=True)
+        gathered = jnp.concatenate(lax.all_gather(by_row, "col"), axis=2)
         unit_block = gathered.reshape(gathered.shape[0], gathered.shape[1] * gathered.shape[2])
         rates_now = full_rates[step_back]
         noise_list.insert(0, jnp.sum(unit_block, axis=0))

time: 642 us -> 640 us (level)
  no operation moved by 1% of the time
where the time goes in v1:
time: 640 us; the launch traced here: 632 us
  waiting for transfers between devices  213 us (33%)
  matrix products  212 us (33%)
  blocking collectives  109 us (17%)
  other arithmetic  48.9 us (8%)
  local copies, waits for them, and re-layouts  33.1 us (5%)
  between operations  14.6 us (2%)
    dot_general x3, matrix products, shards(): lax.dot_general(unit_block, rates_now, (((0,), (0,)), ((), ())), precisio...  112 us
    dot_general x3, matrix products, shards(): jnp.dot(unit_block, weight, precision=lax.Precision.HIGHEST, preferred_el...  101 us
    reduce_scatter x3, waiting for transfers between devices, shards(): lax.psum_scatter(partial_sum, 'row', scatter_dimension=0, tiled=True)  86.8 us
    all_gather x3, waiting for transfers between devices, shards(): gathered = jnp.concatenate(lax.all_gather(by_row, 'col'), axis=2)  68.6 us
    all_to_all x3, blocking collectives, shards(): lax.all_to_all(by_col, 'row', split_axis=1, concat_axis=0, tiled=True)  67.2 us
    all_gather x1, waiting for transfers between devices, shards(): full_rates = lax.all_gather(rates, 'row', axis=1, tiled=True)  57.2 us
    all_to_all x3, blocking collectives, shards(): lax.all_to_all(spread, 'col', split_axis=2, concat_axis=1, tiled=True)  41.9 us
    unnamed x3, other arithmetic  29 us
  transfers between devices with their start and end apart: 7, of which 5 were waited for; matrix products, arithmetic and copies ran while one was open for 22% of the time, Pallas kernels for 0%

profile of v1, /device:TPU:0, one launch (start us, length us, event | category | flops | bytes accessed | tf_op | source)
XLA Modules:
  0.0 632.0 jit_solution(6161665524848957625)
XLA Ops:
  9.0 14.7 %all_to_all.99 = f32[64,256,8]{1,0,2:T(8,128)S(1)} all-to-all(f32[64,256,8]{1,0,2:T(8,128)S(1)} %copy.20), channel_id=1, replica_groups=mesh['row'=4,'col'=8] {'col'}, dimensions={2} | all-to-all | bytes 1048576 | tf_op jit(solution)/shard_map/all_to_all | solution.py:20
  24.6 9.3 %reduce.3 = f32[2048,64]{1,0:T(8,128)S(1)} reduce(f32[2048,1,64]{2,1,0:T(1,128)S(1)} %bitcast.84, f32[]{:T(128)} %broadcast.24), dimensions={1}, to_apply=%bitcast.73.reduce_sub_computation | reduce | bytes 1048580
  34.6 18.6 %all_to_all.100 = f32[4,1,32768]{2,1,0:T(1,128)S(1)} all-to-all(f32[4,1,32768]{2,1,0:T(1,128)S(1)} %reshape.51), channel_id=1, replica_groups=mesh['row'=4,'col'=8] {'row'}, dimensions={0} | all-to-all | bytes 1048576 | tf_op jit(solution)/shard_map/all_to_all | solution.py:21
  53.2 2.1 reduce.4
  58.3 34.2 %all-gather.5.cloned.1.call-done = f32[8,256,512,1]{2,1,3,0:T(8,128)} async-done(((f32[1,256,512,1]{2,1,3,0:T(8,128)}), f32[8,256,512,1]{2,1,3,0:T(8,128)}) %all-gather.5.cloned.1.call-update) | async-done | bytes 4194320 | tf_op jit(solution)/shard_map/all_gather | solution.py:22
  92.6 5.4 copy.25
  98.0 33.8 %fusion.9 = f32[256,2048]{1,0:T(8,128)} fusion(f32[4096,2048]{1,0:T(8,128)} %param.4, f32[8,256,512,1]{1,0,2,3:T(8,128)} %copy.25), kind=kOutput, calls=%fused_computation.10 | convolution fusion | flops 25769803776 | bytes 39845888 | tf_op jit(solution)/shard_map/dot_general | solution.py:33
  132.0 43.7 %reduce-scatter.4.cloned.1.call-done = f32[64,2048]{1,0:T(8,128)} async-done(((f32[256,2048]{1,0:T(8,128)}), f32[64,2048]{1,0:T(8,128)}) %reduce-scatter.4.cloned.1.call-update) | async-done | bytes 524304 | tf_op jit(solution)/shard_map/reduce_scatter | solution.py:36
  177.7 13.7 %all_to_all.101 = f32[64,256,8]{1,0,2:T(8,128)S(1)} all-to-all(f32[64,256,8]{1,0,2:T(8,128)S(1)} %copy.27), channel_id=1, replica_groups=mesh['row'=4,'col'=8] {'col'}, dimensions={2} | all-to-all | bytes 1048576 | tf_op jit(solution)/shard_map/all_to_all | solution.py:20
  191.7 9.3 %reduce.5 = f32[2048,64]{1,0:T(8,128)S(1)} reduce(f32[2048,1,64]{2,1,0:T(1,128)S(1)} %bitcast.85, f32[]{:T(128)} %broadcast.24), dimensions={1}, to_apply=%bitcast.75.reduce_sub_computation | reduce | bytes 1048580
  201.8 16.6 %all_to_all.102 = f32[4,1,32768]{2,1,0:T(1,128)S(1)} all-to-all(f32[4,1,32768]{2,1,0:T(1,128)S(1)} %reshape.53), channel_id=1, replica_groups=mesh['row'=4,'col'=8] {'row'}, dimensions={0} | all-to-all | bytes 1048576 | tf_op jit(solution)/shard_map/all_to_all | solution.py:21
  218.4 2.1 reduce.6
  223.4 34.3 %all-gather.7.cloned.1.call-done = f32[8,256,512,1]{2,1,3,0:T(8,128)} async-done(((f32[1,256,512,1]{2,1,3,0:T(8,128)}), f32[8,256,512,1]{2,1,3,0:T(8,128)}) %all-gather.7.cloned.1.call-update) | async-done | bytes 4194320 | tf_op jit(solution)/shard_map/all_gather | solution.py:22
  257.8 5.5 copy.32
  263.2 33.9 %fusion.5 = f32[256,2048]{1,0:T(8,128)} fusion(f32[4096,2048]{1,0:T(8,128)} %param.4, f32[8,256,512,1]{1,0,2,3:T(8,128)} %copy.32), kind=kOutput, calls=%fused_computation.6 | convolution fusion | flops 25769803776 | bytes 39845888 | tf_op jit(solution)/shard_map/dot_general | solution.py:33
  297.8 43.1 %reduce-scatter.6.cloned.1.call-done = f32[64,2048]{1,0:T(8,128)} async-done(((f32[256,2048]{1,0:T(8,128)}), f32[64,2048]{1,0:T(8,128)}) %reduce-scatter.6.cloned.1.call-update) | async-done | bytes 524304 | tf_op jit(solution)/shard_map/reduce_scatter | solution.py:36
  340.9 2.0 broadcast_multiply_fusion
  343.7 13.5 %all_to_all.103 = f32[64,256,8]{1,0,2:T(8,128)} all-to-all(f32[64,256,8]{1,0,2:T(8,128)S(1)} %copy.34), channel_id=1, replica_groups=mesh['row'=4,'col'=8] {'col'}, dimensions={2} | all-to-all | bytes 1048576 | tf_op jit(solution)/shard_map/all_to_all | solution.py:20
  357.1 1.4 copy.50
  358.5 10.3 %reduce.7 = f32[2048,64]{1,0:T(8,128)} reduce(f32[2048,1,64]{2,1,0:T(1,128)S(1)} %bitcast.86, f32[]{:T(128)} %broadcast.24), dimensions={1}, to_apply=%bitcast.77.reduce_sub_computation | reduce | bytes 1048580
  368.8 1.9 reshape.55
  370.7 32.0 %all_to_all.104 = f32[4,1,32768]{2,1,0:T(1,128)S(1)} all-to-all(f32[4,1,32768]{2,1,0:T(1,128)S(1)} %reshape.55), channel_id=1, replica_groups=mesh['row'=4,'col'=8] {'row'}, dimensions={0} | all-to-all | bytes 1048576 | tf_op jit(solution)/shard_map/all_to_all | solution.py:21
  402.7 2.1 reduce.8
  407.8 2.8 bitcast_reduce_fusion.2
  410.8 57.2 %all-gather.11.cloned.1.call-done = f32[3,256,2048]{2,1,0:T(8,128)} async-done(((f32[3,64,2048]{2,1,0:T(8,128)}), f32[3,256,2048]{2,1,0:T(8,128)}) %all-gather.11.cloned.1.call-update) | async-done | bytes 6291472 | tf_op jit(solution)/shard_map/all_gather | solution.py:13
  468.0 32.5 %fusion.7 = f32[4096,2048]{1,0:T(8,128)} fusion(f32[8,256,512,1]{1,0,2,3:T(8,128)} %copy.25, f32[3,256,2048]{2,1,0:T(8,128)} %all-gather.11.cloned.1.call-done), kind=kOutput, calls=%fused_computation.8 | convolution fusion | flops 25769803776 | bytes 39845888 | tf_op jit(solution)/shard_map/dot_general | solution.py:26
  501.3 32.7 %fusion.3 = f32[4096,2048]{1,0:T(8,128)} fusion(f32[8,256,512,1]{1,0,2,3:T(8,128)} %copy.32, f32[3,256,2048]{2,1,0:T(8,128)} %all-gather.11.cloned.1.call-done), kind=kOutput, calls=%fused_computation.4 | convolution fusion | flops 25769803776 | bytes 39845888 | tf_op jit(solution)/shard_map/dot_general | solution.py:26
  534.0 5.5 copy.39
  539.5 3.0 bitcast_reduce_fusion
  543.0 32.8 %fusion.1 = f32[256,2048]{1,0:T(8,128)} fusion(f32[4096,2048]{1,0:T(8,128)} %param.4, f32[8,256,512,1]{1,0,2,3:T(8,128)S(1)} %copy-done), kind=kOutput, calls=%fused_computation.2 | convolution fusion | flops 25769803776 | bytes 39845888 | tf_op jit(solution)/shard_map/dot_general | solution.py:33
  576.7 46.3 %add_add_fusion = f32[4096,2048]{1,0:T(8,128)} fusion(f32[4096,2048]{1,0:T(8,128)} %fusion.7, f32[4096,2048]{1,0:T(8,128)} %fusion.3, f32[8,256,512,1]{1,0,2,3:T(8,128)} %copy.39, f32[3,256,2048]{2,1,0:T(8,128)} %all-gather.11.cloned.1.call-done), kind=kOutput, calls=%fused_computation | convolution fusion | flops 25786580992 | bytes 106954752 | tf_op jit(solution)/shard_map/dot_general | solution.py:26
  623.0 1.9 fusion.11
  (58 shorter events, 18.8 us)
Async XLA Ops:
  7.2 85.4 %all-gather.5.cloned.1.call-start = ((), (), s32[]{:S(2)}) async-start(), calls=%async_computation.9 | async-start | bytes 4718592 | tf_op jit(solution)/shard_map/all_gather | solution.py:22
  58.0 117.7 %reduce-scatter.4.cloned.1.call-start = ((), (), s32[]{:S(2)}) async-start(), calls=%async_computation.10 | async-start | bytes 2621440 | tf_op jit(solution)/shard_map/reduce_scatter | solution.py:36
  98.0 33.9 %copy-start.6 = (f32[2048]{0:T(1024)S(1)}, f32[2048]{0:T(1024)}, u32[]{:S(2)}) copy-start(f32[2048]{0:T(1024)} %param.5) | copy-start | bytes 24580
  98.0 77.7 %copy-start.3 = (f32[64,2048]{1,0:T(8,128)S(1)}, f32[64,2048]{1,0:T(8,128)}, u32[]{:S(2)}) copy-start(f32[64,2048]{1,0:T(8,128)} %param.7) | copy-start | bytes 1572868
  131.9 125.9 %all-gather.7.cloned.1.call-start = ((), (), s32[]{:S(2)}) async-start(), calls=%async_computation.11 | async-start | bytes 4718592 | tf_op jit(solution)/shard_map/all_gather | solution.py:22
  223.2 117.7 %reduce-scatter.6.cloned.1.call-start = ((), (), s32[]{:S(2)}) async-start(), calls=%async_computation.12 | async-start | bytes 2621440 | tf_op jit(solution)/shard_map/reduce_scatter | solution.py:36
  263.2 77.6 %copy-start.5 = (f32[64,2048]{1,0:T(8,128)S(1)}, f32[64,2048]{1,0:T(8,128)}, u32[]{:S(2)}) copy-start(f32[64,2048]{1,0:T(8,128)} %reduce-scatter.4.cloned.1.call-done) | copy-start | bytes 1572868
  297.1 43.8 %copy-start.2 = (f32[3,64,2048]{2,1,0:T(8,128)S(1)}, f32[3,64,2048]{2,1,0:T(8,128)}, u32[]{:S(2)}) copy-start(f32[3,64,2048]{2,1,0:T(8,128)} %param.6) | copy-start | bytes 4718596
  297.1 170.9 %all-gather.11.cloned.1.call-start = ((), (), s32[]{:S(2)}) async-start(), calls=%async_computation.15 | async-start | bytes 7864320 | tf_op jit(solution)/shard_map/all_gather | solution.py:13
  297.7 236.3 %all-gather.9.cloned.1.call-start = ((), (), s32[]{:S(2)}) async-start(), calls=%async_computation.13 | async-start | bytes 4718592 | tf_op jit(solution)/shard_map/all_gather | solution.py:22
  407.5 215.5 %reduce-scatter.8.cloned.1.call-start = ((), (), s32[]{:S(2)}) async-start(), calls=%async_computation.14 | async-start | bytes 2621440 | tf_op jit(solution)/shard_map/reduce_scatter | solution.py:36
  468.0 32.5 %copy-start.1 = (f32[8,256,512,1]{1,0,2,3:T(8,128)S(1)}, f32[8,256,512,1]{1,0,2,3:T(8,128)}, u32[]{:S(2)}) copy-start(f32[8,256,512,1]{1,0,2,3:T(8,128)} %copy.32) | copy-start | bytes 12582916
  539.5 3.4 copy-start
  576.7 46.3 %copy-start.4 = (f32[64,2048]{1,0:T(8,128)S(1)}, f32[64,2048]{1,0:T(8,128)}, u32[]{:S(2)}) copy-start(f32[64,2048]{1,0:T(8,128)} %get-tuple-element.4) | copy-start | bytes 1572868
Sparse Core Ops, SparseCore 0:
  58.1 34.4 all-gather.4
  132.0 43.6 reduce-scatter.3
  223.3 34.4 all-gather.6
  297.2 43.5 reduce-scatter.5
  342.3 125.6 all-gather.10
  469.7 34.7 all-gather.8
  576.1 41.8 reduce-scatter.7
